TPU v7x, 32 devices: a whole 2x2x4 slice. The times are simulated.
32 devices in a mesh: team: 4 (over z), blk: 4 (over y, x), head: 2 (over core).
Axes of the slice: x: 2, y: 2, z: 4, core: 2. Of those that a mesh axis runs over, the one named last changes fastest.
Arguments:
- query: bfloat16 [2048, 2560], P(('team', 'blk'), 'head'), parts along dimension 1, may hold values from -15 to 15
- keys: bfloat16 [2048, 2560], P(('team', 'blk'), 'head'), parts along dimension 1, may hold values from -6 to 6
- values: bfloat16 [2048, 2560], P(('team', 'blk'), 'head'), parts along dimension 1, may hold values from -6 to 6
Outputs:
- attended: bfloat16 [2048, 2560], P(('team', 'blk'), 'head'), parts along dimension 1
There are 2 independent parts, one for each index of `head`. A program takes and returns all parts, laid end to end along the dimension named above; each array names one. Nothing has to cross between parts.
All inputs are finite; a program needn't handle non-finite values.
Results may differ from a plain program's by a relative error of at most 0.006.
Values may be sent and summed in bfloat16 or wider, within the bound.
A program may use at most 128 MiB of HBM per device.

v0:
```python
import math

import jax
import jax.numpy as jnp
from jax import lax
from jax.sharding import PartitionSpec as P

HEAD_DIM = 128


def shifted(value, axis, by):
    count = lax.axis_size(axis)
    return lax.ppermute(value, axis, [(i, (i + by) % count) for i in range(count)])


def on_device(query, keys, values):
    shard_rows = query.shape[0]
    feature_width = query.shape[1]
    head_count = feature_width // HEAD_DIM
    score_scale = 1.0 / math.sqrt(HEAD_DIM)
    team_query = lax.all_gather(query, "team", axis=0, tiled=True)
    team_heads = team_query.reshape(-1, head_count, HEAD_DIM)

    def scores_of(key_block):
        key_heads = key_block.reshape(shard_rows, head_count, HEAD_DIM)
        return (
            jnp.einsum("qhd,khd->qhk", team_heads, key_heads, preferred_element_type=jnp.float32)
            * score_scale
        )

    def weighted(weights, value_block):
        value_heads = value_block.reshape(shard_rows, head_count, HEAD_DIM)
        return jnp.einsum(
            "qhk,khd->qhd",
            weights.astype(jnp.bfloat16),
            value_heads,
            preferred_element_type=jnp.float32,
        )

    def absorb(state, key_block, value_block):
        row_peak, row_total, accumulated = state
        scores = scores_of(key_block)
        new_peak = jnp.maximum(row_peak, jnp.max(scores, axis=2))
        rescale = jnp.exp(row_peak - new_peak)
        weights = jnp.exp(scores - new_peak[..., None])
        row_total = row_total * rescale + jnp.sum(weights, axis=2)
        accumulated = accumulated * rescale[..., None] + weighted(weights, value_block)
        return (new_peak, row_total, accumulated)

    first_scores = scores_of(keys)
    first_peak = jnp.max(first_scores, axis=2)
    first_weights = jnp.exp(first_scores - first_peak[..., None])
    state = (first_peak, jnp.sum(first_weights, axis=2), weighted(first_weights, values))

    def step_ahead(key_block, value_block):
        return shifted((key_block, value_block), "blk", 1)

    def step_behind(key_block, value_block):
        return shifted((key_block, value_block), "blk", -1)

    block_count = lax.axis_size("blk")

    def one_turn(turn_index, carried):
        ahead_keys, ahead_values, behind_keys, behind_values, inner = carried
        ahead_keys, ahead_values = step_ahead(ahead_keys, ahead_values)
        behind_keys, behind_values = step_behind(behind_keys, behind_values)
        inner = absorb(inner, ahead_keys, ahead_values)
        inner = absorb(inner, behind_keys, behind_values)
        return (ahead_keys, ahead_values, behind_keys, behind_values, inner)

    carried = lax.fori_loop(0, block_count // 2 - 1, one_turn, (keys, values, keys, values, state))
    last_keys, last_values = step_ahead(carried[0], carried[1])
    row_peak, row_total, accumulated = absorb(carried[4], last_keys, last_values)
    peaks, totals, sums = (
        lax.all_to_all(row_peak[None], "team", split_axis=1, concat_axis=0, tiled=True),
        lax.all_to_all(row_total[None], "team", split_axis=1, concat_axis=0, tiled=True),
        lax.all_to_all(accumulated[None], "team", split_axis=1, concat_axis=0, tiled=True),
    )
    joint_peak = jnp.max(peaks, axis=0)
    rescale = jnp.exp(peaks - joint_peak[None])
    own_total = jnp.sum(totals * rescale, axis=0)
    own_sum = jnp.sum(sums * rescale[..., None], axis=0)
    attended = (own_sum / own_total[..., None]).astype(jnp.bfloat16)
    return attended.reshape(shard_rows, feature_width)


def solution(mesh):
    placed = (P(("team", "blk"), "head"), P(("team", "blk"), "head"), P(("team", "blk"), "head"))
    return jax.shard_map(
        on_device, mesh=mesh, in_specs=placed, out_specs=P(("team", "blk"), "head"), check_vma=False
    )
```

profile of v0, /device:TPU:0, one launch (start us, length us, event | category | flops | bytes accessed | tf_op | source)
XLA Modules:
  0.0 162.7 jit_solution(10376589958835616199)
XLA Ops:
  6.5 1.9 %copy.106 = bf16[128,1280]{0,1:T(8,128)(2,1)} copy(bf16[128,1280]{1,0:T(8,128)(2,1)} %param.3) | data formatting | bytes 655360 | tf_op args[0]
  8.4 1.2 copy.105
  9.6 3.0 %collective-permute-start = (bf16[128,1280]{0,1:T(8,128)(2,1)S(1)}, bf16[128,1280]{0,1:T(8,128)(2,1)S(1)}, u32[]{:S(2)}, u32[]{:S(2)}) collective-permute-start(bf16[128,1280]{0,1:T(8,128)(2,1)S(1)} %copy.105), channel_id=1, source_target_pairs={{0,2},{2,4},{4,6},{6,0},{1,3},{3,5},{5,7},{7,1},{8,10},{10,12},{12... | collective-permute-start | bytes 983048 | tf_op jit(solution)/shard_map/while/body/eval_jaxpr/ppermute | solution.py:13
  12.6 1.2 copy.109
  13.8 1.5 collective-permute-start.1
  15.4 1.4 collective-permute-start.2
  16.9 5.2 %collective-permute-done = bf16[128,1280]{0,1:T(8,128)(2,1)S(1)} collective-permute-done((bf16[128,1280]{0,1:T(8,128)(2,1)S(1)}, bf16[128,1280]{0,1:T(8,128)(2,1)S(1)}, u32[]{:S(2)}, u32[]{:S(2)}) %collective-permute-start) | collective-permute-done | bytes 327712 | tf_op jit(solution)/shard_map/while/body/eval_jaxpr/ppermute | solution.py:13
  22.1 1.1 collective-permute-start.4
  23.2 6.1 %collective-permute-done.1 = bf16[128,1280]{0,1:T(8,128)(2,1)} collective-permute-done((bf16[128,1280]{0,1:T(8,128)(2,1)S(1)}, bf16[128,1280]{0,1:T(8,128)(2,1)}, u32[]{:S(2)}, u32[]{:S(2)}) %collective-permute-start.1) | collective-permute-done | bytes 327712 | tf_op jit(solution)/shard_map/while/body/eval_jaxpr/ppermute | solution.py:13
  29.3 1.1 collective-permute-start.5
  30.3 14.8 %all-gather.2.cloned.1.call-done = bf16[512,1280]{0,1:T(8,128)(2,1)} async-done(((bf16[128,1280]{0,1:T(8,128)(2,1)}), bf16[512,1280]{0,1:T(8,128)(2,1)}) %all-gather.2.cloned.1.call-update) | async-done | bytes 1310736 | tf_op jit(solution)/shard_map/all_gather | solution.py:21
  45.1 2.0 %bitcast_reduce_fusion.3 = (f32[512,10]{0,1:T(8,128)S(1)}, f32[10,128,512]{2,1,0:T(8,128)S(1)}) fusion(bf16[128,10,128]{0,2,1:T(8,128)(2,1)S(1)} %bitcast.149, bf16[512,10,128]{0,2,1:T(8,128)(2,1)} %bitcast.142), kind=kOutput, calls=%fused_computation.17 | convolution fusion | flops 169077760 | bytes 4280320 | tf_op jit(solution)/shard_map/qhd,khd->qhk/dot_general | solution.py:27
  47.1 0.6 bitcast_reduce_fusion.2
  47.7 0.6 bitcast_reduce_fusion.1
  48.3 1.9 %collective-permute-done.4 = bf16[128,1280]{0,1:T(8,128)(2,1)S(1)} collective-permute-done((bf16[128,1280]{0,1:T(8,128)(2,1)S(1)}, bf16[128,1280]{0,1:T(8,128)(2,1)S(1)}, u32[]{:S(2)}, u32[]{:S(2)}) %collective-permute-start.4) | collective-permute-done | bytes 327712 | tf_op jit(solution)/shard_map/ppermute | solution.py:13
  50.2 0.7 copy-done.7
  51.0 1.5 bitcast_reduce_fusion
  52.5 0.6 subtract_exponential_fusion.2
  53.1 0.6 subtract_exponential_fusion.1
  53.8 0.6 subtract_exponential_fusion
  54.4 0.5 fusion.11
  54.9 1.0 fusion.7
  55.9 0.5 fusion.13
  56.3 0.6 bitcast_maximum_fusion
  57.1 0.6 broadcast.52
  57.7 1.3 reduce.2
  59.0 0.8 reshape.207
  59.8 5.3 %all-to-all-start.1 = ((f32[4,1,1280]{2,1,0:T(1,128)}), f32[4,1,1280]{2,1,0:T(1,128)S(1)}, u32[]{:S(2)}, u32[]{:S(2)}) async-start(f32[4,1,1280]{2,1,0:T(1,128)} %reshape.207), calls=%async_computation.1 | async-start | bytes 40960 | tf_op jit(solution)/shard_map/all_to_all | solution.py:75
  65.1 4.2 %fusion.16 = f32[10,512,128]{2,1,0:T(8,128)} fusion(bf16[128,10,128]{0,2,1:T(8,128)(2,1)} %bitcast.11, f32[10,128,512]{2,1,0:T(8,128)} %copy-done.4, f32[512,10]{0,1:T(8,128)} %copy-done.6), kind=kOutput, calls=%fused_computation.28 | convolution fusion | flops 169738240 | bytes 5591040 | tf_op jit(solution)/shard_map/while/body/eval_jaxpr/qhk,khd->qhd/dot_general | solution.py:33
  69.3 3.3 %fusion.18 = f32[10,512,128]{2,1,0:T(8,128)} fusion(bf16[128,10,128]{0,2,1:T(8,128)(2,1)} %bitcast.7, f32[10,128,512]{2,1,0:T(8,128)S(1)} %copy-done.3, f32[512,10]{0,1:T(8,128)S(1)} %get-tuple-element.24), kind=kOutput, calls=%fused_computation.29 | convolution fusion | flops 169738240 | bytes 5591040 | tf_op jit(solution)/shard_map/while/body/eval_jaxpr/qhk,khd->qhd/dot_general | solution.py:33
  72.7 2.2 %fusion.20 = f32[10,512,128]{2,1,0:T(8,128)} fusion(bf16[128,10,128]{0,2,1:T(8,128)(2,1)S(1)} %bitcast.151, f32[10,128,512]{2,1,0:T(8,128)S(1)} %copy-done.1, f32[512,10]{0,1:T(8,128)S(1)} %get-tuple-element.42), kind=kOutput, calls=%fused_computation.30 | convolution fusion | flops 169738240 | bytes 5591040 | tf_op jit(solution)/shard_map/qhk,khd->qhd/dot_general | solution.py:33
  74.9 0.1 copy.132
  75.0 1.3 reduce
  76.3 0.8 reshape.209
  77.1 5.1 %all-to-all-start.2 = ((f32[4,1,1280]{2,1,0:T(1,128)}), f32[4,1,1280]{2,1,0:T(1,128)S(1)}, u32[]{:S(2)}, u32[]{:S(2)}) async-start(f32[4,1,1280]{2,1,0:T(1,128)} %reshape.209), calls=%async_computation.2 | async-start | bytes 40960 | tf_op jit(solution)/shard_map/all_to_all | solution.py:76
  82.2 5.5 %fusion = f32[1,512,10,128]{3,1,2,0:T(8,128)S(1)} fusion(f32[10,512,128]{2,1,0:T(8,128)} %fusion.16, f32[10,512,128]{2,1,0:T(8,128)} %fusion.18, f32[10,512,128]{2,1,0:T(8,128)} %fusion.20, bf16[128,10,128]{0,2,1:T(8,128)(2,1)} %bitcast.15, f32[10,128,512]{2,1,0:T(8,128)S(1)} %get-tuple-element.49, f32[512,10]{0,1:T(8,128)S(1)} %copy-done.9, ...), kind=kOutput, calls=%fused_computation.1 | convolution fusion | flops 173670400 | bytes 13516800 | tf_op jit(solution)/shard_map/qhk,khd->qhd/dot_general | solution.py:33
  87.7 4.2 %copy.128 = f32[1,512,10,128]{3,0,2,1:T(1,128)} copy(f32[1,512,10,128]{3,1,2,0:T(8,128)S(1)} %fusion) | data formatting | bytes 5242880 | tf_op jit(solution)/shard_map/broadcast_in_dim | solution.py:77
  92.0 5.1 %all-to-all-start = ((f32[1,512,10,128]{3,0,2,1:T(1,128)}), f32[1,512,10,128]{3,0,2,1:T(1,128)S(1)}, u32[]{:S(2)}, u32[]{:S(2)}) async-start(f32[1,512,10,128]{3,0,2,1:T(1,128)} %copy.128), calls=%async_computation | async-start | bytes 5242880 | tf_op jit(solution)/shard_map/all_to_all | solution.py:77
  97.0 0.7 reduce.3
  97.7 0.4 reshape.208
  98.3 0.7 reduce.1
  99.0 0.4 reshape.210
  99.6 53.8 %all-to-all-done = f32[1,512,10,128]{3,0,2,1:T(1,128)S(1)} async-done(((f32[1,512,10,128]{3,0,2,1:T(1,128)}), f32[1,512,10,128]{3,0,2,1:T(1,128)S(1)}, u32[]{:S(2)}, u32[]{:S(2)}) %all-to-all-start) | async-done | bytes 2621472 | tf_op jit(solution)/shard_map/all_to_all | solution.py:77
  153.4 0.2 copy.129
  153.6 0.9 multiply_reduce_fusion
  154.5 0.2 divide_convert_fusion
  154.7 0.2 copy.134
  154.9 0.9 copy.135
  (41 shorter events, 0.7 us)
Async XLA Ops:
  6.5 38.6 %all-gather.2.cloned.1.call-start = ((), (), s32[]{:S(2)}) async-start(), calls=%async_computation.3 | async-start | bytes 1638400 | tf_op jit(solution)/shard_map/all_gather | solution.py:21
  9.6 12.5 %collective-permute-start = (bf16[128,1280]{0,1:T(8,128)(2,1)S(1)}, bf16[128,1280]{0,1:T(8,128)(2,1)S(1)}, u32[]{:S(2)}, u32[]{:S(2)}) collective-permute-start(bf16[128,1280]{0,1:T(8,128)(2,1)S(1)} %copy.105), channel_id=1, source_target_pairs={{0,2},{2,4},{4,6},{6,0},{1,3},{3,5},{5,7},{7,1},{8,10},{10,12},{12... | collective-permute-start | bytes 983048 | tf_op jit(solution)/shard_map/while/body/eval_jaxpr/ppermute | solution.py:13
  13.8 15.5 %collective-permute-start.1 = (bf16[128,1280]{0,1:T(8,128)(2,1)S(1)}, bf16[128,1280]{0,1:T(8,128)(2,1)}, u32[]{:S(2)}, u32[]{:S(2)}) collective-permute-start(bf16[128,1280]{0,1:T(8,128)(2,1)S(1)} %copy.109), channel_id=1, source_target_pairs={{0,2},{2,4},{4,6},{6,0},{1,3},{3,5},{5,7},{7,1},{8,10},{10,12},{12... | collective-permute-start | bytes 983048 | tf_op jit(solution)/shard_map/while/body/eval_jaxpr/ppermute | solution.py:13
  15.4 32.4 %collective-permute-start.2 = (bf16[128,1280]{0,1:T(8,128)(2,1)S(1)}, bf16[128,1280]{0,1:T(8,128)(2,1)S(1)}, u32[]{:S(2)}, u32[]{:S(2)}) collective-permute-start(bf16[128,1280]{0,1:T(8,128)(2,1)S(1)} %copy.105), channel_id=1, source_target_pairs={{0,6},{2,0},{4,2},{6,4},{1,7},{3,1},{5,3},{7,5},{8,14},{10,8},{12,... | collective-permute-start | bytes 983048 | tf_op jit(solution)/shard_map/while/body/eval_jaxpr/ppermute | solution.py:13
  16.8 48.3 %collective-permute-start.3 = (bf16[128,1280]{0,1:T(8,128)(2,1)S(1)}, bf16[128,1280]{0,1:T(8,128)(2,1)}, u32[]{:S(2)}, u32[]{:S(2)}) collective-permute-start(bf16[128,1280]{0,1:T(8,128)(2,1)S(1)} %copy.109), channel_id=1, source_target_pairs={{0,6},{2,0},{4,2},{6,4},{1,7},{3,1},{5,3},{7,5},{8,14},{10,8},{12,... | collective-permute-start | bytes 983048 | tf_op jit(solution)/shard_map/while/body/eval_jaxpr/ppermute | solution.py:13
  22.1 28.1 %collective-permute-start.4 = (bf16[128,1280]{0,1:T(8,128)(2,1)S(1)}, bf16[128,1280]{0,1:T(8,128)(2,1)S(1)}, u32[]{:S(2)}, u32[]{:S(2)}) collective-permute-start(bf16[128,1280]{0,1:T(8,128)(2,1)S(1)} %collective-permute-done), channel_id=1, source_target_pairs={{0,2},{2,4},{4,6},{6,0},{1,3},{3,5},{5,7},{7,1},{8,10},{10,12},{12... | collective-permute-start | bytes 983048 | tf_op jit(solution)/shard_map/ppermute | solution.py:13
  29.3 52.9 %collective-permute-start.5 = (bf16[128,1280]{0,1:T(8,128)(2,1)}, bf16[128,1280]{0,1:T(8,128)(2,1)}, u32[]{:S(2)}, u32[]{:S(2)}) collective-permute-start(bf16[128,1280]{0,1:T(8,128)(2,1)} %collective-permute-done.1), channel_id=1, source_target_pairs={{0,2},{2,4},{4,6},{6,0},{1,3},{3,5},{5,7},{7,1},{8,10},{10,12},{12... | collective-permute-start | bytes 983048 | tf_op jit(solution)/shard_map/ppermute | solution.py:13
  45.1 2.0 %copy-start.5 = (bf16[512,1280]{0,1:T(8,128)(2,1)S(1)}, bf16[512,1280]{0,1:T(8,128)(2,1)}, u32[]{:S(2)}) copy-start(bf16[512,1280]{0,1:T(8,128)(2,1)} %all-gather.2.cloned.1.call-done) | copy-start | bytes 3932164
  47.1 7.8 %copy-start = (f32[10,128,512]{2,1,0:T(8,128)}, f32[10,128,512]{2,1,0:T(8,128)S(1)}, u32[]{:S(2)}) copy-start(f32[10,128,512]{2,1,0:T(8,128)S(1)} %get-tuple-element.43) | copy-start | bytes 7864324
  47.7 7.2 %copy-start.2 = (f32[10,128,512]{2,1,0:T(8,128)}, f32[10,128,512]{2,1,0:T(8,128)S(1)}, u32[]{:S(2)}) copy-start(f32[10,128,512]{2,1,0:T(8,128)S(1)} %get-tuple-element.45) | copy-start | bytes 7864324
  48.3 6.5 %copy-start.4 = (f32[10,128,512]{2,1,0:T(8,128)}, f32[10,128,512]{2,1,0:T(8,128)S(1)}, u32[]{:S(2)}) copy-start(f32[10,128,512]{2,1,0:T(8,128)S(1)} %get-tuple-element.47) | copy-start | bytes 7864324
  50.2 0.7 copy-start.7
  53.8 2.1 %copy-start.6 = (f32[512,10]{0,1:T(8,128)}, f32[512,10]{0,1:T(8,128)S(1)}, u32[]{:S(2)}) copy-start(f32[512,10]{0,1:T(8,128)S(1)} %get-tuple-element.26) | copy-start | bytes 61444
  54.4 1.5 copy-start.8
  59.8 17.3 %all-to-all-start.1 = ((f32[4,1,1280]{2,1,0:T(1,128)}), f32[4,1,1280]{2,1,0:T(1,128)S(1)}, u32[]{:S(2)}, u32[]{:S(2)}) async-start(f32[4,1,1280]{2,1,0:T(1,128)} %reshape.207), calls=%async_computation.1 | async-start | bytes 40960 | tf_op jit(solution)/shard_map/all_to_all | solution.py:75
  65.1 4.2 %copy-start.3 = (f32[10,128,512]{2,1,0:T(8,128)S(1)}, f32[10,128,512]{2,1,0:T(8,128)}, u32[]{:S(2)}) copy-start(f32[10,128,512]{2,1,0:T(8,128)} %copy-done.2) | copy-start | bytes 7864324
  69.3 3.3 %copy-start.1 = (f32[10,128,512]{2,1,0:T(8,128)S(1)}, f32[10,128,512]{2,1,0:T(8,128)}, u32[]{:S(2)}) copy-start(f32[10,128,512]{2,1,0:T(8,128)} %copy-done) | copy-start | bytes 7864324
  72.6 2.3 %copy-start.13 = (f32[1,512,10]{1,2,0:T(8,128)S(1)}, f32[1,512,10]{1,2,0:T(8,128)}, u32[]{:S(2)}) copy-start(f32[1,512,10]{1,2,0:T(8,128)} %get-tuple-element.41) | copy-start | bytes 61444
  72.6 9.6 %copy-start.9 = (f32[512,10]{0,1:T(8,128)S(1)}, f32[512,10]{0,1:T(8,128)}, u32[]{:S(2)}) copy-start(f32[512,10]{0,1:T(8,128)} %copy-done.8) | copy-start | bytes 61444
  72.6 9.6 %copy-start.10 = (f32[512,10]{0,1:T(8,128)S(1)}, f32[512,10]{0,1:T(8,128)}, u32[]{:S(2)}) copy-start(f32[512,10]{0,1:T(8,128)} %get-tuple-element.23) | copy-start | bytes 61444
  72.6 9.6 %copy-start.11 = (f32[512,10]{0,1:T(8,128)S(1)}, f32[512,10]{0,1:T(8,128)}, u32[]{:S(2)}) copy-start(f32[512,10]{0,1:T(8,128)} %get-tuple-element.25) | copy-start | bytes 61444
  72.6 9.6 %copy-start.12 = (f32[512,10]{0,1:T(8,128)S(1)}, f32[512,10]{0,1:T(8,128)}, u32[]{:S(2)}) copy-start(f32[512,10]{0,1:T(8,128)} %get-tuple-element.36) | copy-start | bytes 61444
  77.1 14.8 %all-to-all-start.2 = ((f32[4,1,1280]{2,1,0:T(1,128)}), f32[4,1,1280]{2,1,0:T(1,128)S(1)}, u32[]{:S(2)}, u32[]{:S(2)}) async-start(f32[4,1,1280]{2,1,0:T(1,128)} %reshape.209), calls=%async_computation.2 | async-start | bytes 40960 | tf_op jit(solution)/shard_map/all_to_all | solution.py:76
  92.0 61.4 %all-to-all-start = ((f32[1,512,10,128]{3,0,2,1:T(1,128)}), f32[1,512,10,128]{3,0,2,1:T(1,128)S(1)}, u32[]{:S(2)}, u32[]{:S(2)}) async-start(f32[1,512,10,128]{3,0,2,1:T(1,128)} %copy.128), calls=%async_computation | async-start | bytes 5242880 | tf_op jit(solution)/shard_map/all_to_all | solution.py:77
Sparse Core Ops, SparseCore 0:
  8.9 36.1 all-gather.1
where the time goes:
time: 163 us
  waiting for transfers between devices  81.8 us (50%)
  starting transfers between devices  23.8 us (15%)
  matrix products  19.9 us (12%)
  local copies, waits for them, and re-layouts  14 us (9%)
  between operations  13.7 us (8%)
  other arithmetic  9.52 us (6%)
    all_to_all x1, waiting for transfers between devices, on_device(): lax.all_to_all(accumulated[None], 'team', split_axis=1, concat_axis=0, ti...  53.8 us
    dot_general x4, matrix products, weighted(): jnp.einsum('qhk,khd->qhd', weights.astype(jnp.bfloat16), value_heads, pre...  15.2 us
    all_gather x1, waiting for transfers between devices, on_device(): team_query = lax.all_gather(query, 'team', axis=0, tiled=True)  14.8 us
    ppermute x6, waiting for transfers between devices, shifted(): lax.ppermute(value, axis, [(i, (i + by) % count) for i in range(count)])  13.2 us
    ppermute x6, starting transfers between devices, shifted(): lax.ppermute(value, axis, [(i, (i + by) % count) for i in range(count)])  8.25 us
    unnamed x37, local copies, waits for them, and re-layouts  8.02 us
    all_to_all x1, starting transfers between devices, on_device(): lax.all_to_all(row_peak[None], 'team', split_axis=1, concat_axis=0, tiled...  5.34 us
    all_to_all x1, starting transfers between devices, on_device(): lax.all_to_all(row_total[None], 'team', split_axis=1, concat_axis=0, tile...  5.09 us
  transfers between devices with their start and end apart: 10, of which 5 were waited for; matrix products, arithmetic and copies ran while one was open for 24% of the time, Pallas kernels for 0%

commit v1 on v0

v1 whole, which is shorter than its diff:
```python
import functools
import math

import jax
import jax.numpy as jnp
from jax import lax
from jax.experimental import pallas as pl
from jax.experimental.pallas import tpu as pltpu
from jax.sharding import PartitionSpec as P

HEAD_DIM = 128
MESH = pl.DeviceIdType.MESH
RIGHT, LEFT = 0, 1


def merge(o1, s1, o2, s2):
    top = jnp.maximum(s1, s2)
    a1 = jnp.exp2(s1 - top)
    a2 = jnp.exp2(s2 - top)
    total = a1 + a2
    inverse = 1.0 / total
    return o1 * (a1 * inverse) + o2 * (a2 * inverse), top + jnp.log2(total)


def kernel(
    team, blk, q_ref, k_ref, v_ref, out_ref,
    qbuf, kvbuf, part_o, part_s, o_in, s_in, o_out, s_out,
    q_recv, q_send, kv_recv, kv_send, o_recv, o_send, s_recv, s_send,
):
    rows = q_ref.shape[0]
    heads = q_ref.shape[1] // HEAD_DIM
    scale = math.log2(math.e) / math.sqrt(HEAD_DIM)
    t = lax.axis_index("team")
    b = lax.axis_index("blk")
    last = team - 1

    def columns(h):
        return pl.ds(pl.multiple_of(h * HEAD_DIM, HEAD_DIM), HEAD_DIM)

    barrier = pltpu.get_barrier_semaphore()

    @pl.loop(1, blk)
    def _(r):
        pl.semaphore_signal(
            barrier, inc=1, device_id={"blk": lax.rem(b + r, blk)}, device_id_type=MESH
        )

    @pl.when(t > 0)
    def _():
        pl.semaphore_signal(barrier, inc=1, device_id={"team": t - 1}, device_id_type=MESH)

    @pl.when(t < last)
    def _():
        pl.semaphore_signal(barrier, inc=1, device_id={"team": t + 1}, device_id_type=MESH)

    ends = jnp.where(t > 0, 1, 0) + jnp.where(t < last, 1, 0)
    pl.semaphore_wait(barrier, blk - 1 + ends)

    def kv_copy(h, which, r):
        source = (k_ref, v_ref)[which]
        return pltpu.make_async_remote_copy(
            src_ref=source.at[:, columns(h)],
            dst_ref=kvbuf.at[h, which, r],
            send_sem=kv_send.at[which, h],
            recv_sem=kv_recv.at[which, h],
            device_id={"blk": lax.rem(b + r, blk)},
            device_id_type=MESH,
        )

    def q_copy(source, h, j, way):
        target = t + 1 if way == RIGHT else t - 1
        return pltpu.make_async_remote_copy(
            src_ref=source,
            dst_ref=qbuf.at[h, j],
            send_sem=q_send.at[way, h, j],
            recv_sem=q_recv.at[h, j],
            device_id={"team": target},
            device_id_type=MESH,
        )

    def o_copy(h, j, way):
        target = t + 1 if way == RIGHT else t - 1
        return (
            pltpu.make_async_remote_copy(
                src_ref=o_out.at[way, h, j],
                dst_ref=o_in.at[way, h, j],
                send_sem=o_send.at[way, h, j],
                recv_sem=o_recv.at[way, h, j],
                device_id={"team": target},
                device_id_type=MESH,
            ),
            pltpu.make_async_remote_copy(
                src_ref=s_out.at[way, h, j],
                dst_ref=s_in.at[way, h, j],
                send_sem=s_send.at[way, h, j],
                recv_sem=s_recv.at[way, h, j],
                device_id={"team": target},
                device_id_type=MESH,
            ),
        )

    def send_kv(h):
        for which in range(2):
            @pl.loop(1, blk)
            def _(r):
                kv_copy(h, which, r).start()

    def send_own_q(h):
        @pl.when(t > 0)
        def _():
            q_copy(q_ref.at[:, columns(h)], h, t, LEFT).start()

        @pl.when(t < last)
        def _():
            q_copy(q_ref.at[:, columns(h)], h, t, RIGHT).start()

    def wait_here(ref, semaphore):
        pltpu.make_async_copy(ref, ref, semaphore).wait()

    def relay_q(h, distance):
        @pl.when(t + distance <= last)
        def _():
            j = t + distance
            wait_here(qbuf.at[h, j], q_recv.at[h, j])

            @pl.when(t > 0)
            def _():
                q_copy(qbuf.at[h, j], h, j, LEFT).start()

        @pl.when(t - distance >= 0)
        def _():
            j = t - distance
            wait_here(qbuf.at[h, j], q_recv.at[h, j])

            @pl.when(t < last)
            def _():
                q_copy(qbuf.at[h, j], h, j, RIGHT).start()

    group = math.gcd(blk, 4)
    groups = blk // group

    def attend(h):
        qbuf[h, t] = q_ref[:, columns(h)]
        kvbuf[h, 0, 0] = k_ref[:, columns(h)]
        kvbuf[h, 1, 0] = v_ref[:, columns(h)]
        queries = qbuf[h].reshape(team * rows, HEAD_DIM)
        for which in range(2):
            if blk > 1:
                wait_here(kvbuf.at[h, which, pl.ds(1, blk - 1)], kv_recv.at[which, h])

        def scores_of(c):
            keys = kvbuf[h, 0, pl.ds(c * group, group)].reshape(group * rows, HEAD_DIM)
            return lax.dot_general(
                keys, queries, (((1,), (1,)), ((), ())), preferred_element_type=jnp.float32
            )

        def weighted(c, weights):
            block = kvbuf[h, 1, pl.ds(c * group, group)].reshape(group * rows, HEAD_DIM)
            return lax.dot_general(
                block, weights.astype(jnp.bfloat16), (((0,), (0,)), ((), ())),
                preferred_element_type=jnp.float32,
            )

        scores = scores_of(0)
        peak = jnp.max(scores, axis=0, keepdims=True) * scale
        weights = jnp.exp2(scores * scale - peak)
        total = jnp.sum(weights, axis=0, keepdims=True)
        summed = weighted(0, weights)

        def more(c, state):
            peak, total, summed = state
            scores = scores_of(c)
            higher = jnp.maximum(peak, jnp.max(scores, axis=0, keepdims=True) * scale)
            rescale = jnp.exp2(peak - higher)
            weights = jnp.exp2(scores * scale - higher)
            total = total * rescale + jnp.sum(weights, axis=0, keepdims=True)
            summed = summed * rescale + weighted(c, weights)
            return higher, total, summed

        if groups > 1:
            peak, total, summed = lax.fori_loop(1, groups, more, (peak, total, summed))
        attended = summed * (1.0 / total)
        level = peak + jnp.log2(total)
        for j in range(team):
            part_o[h, j] = attended[:, j * rows : (j + 1) * rows]
            part_s[h, j] = level[:, j * rows : (j + 1) * rows]

    def await_partial(h, j, way):
        wait_here(o_in.at[way, h, j], o_recv.at[way, h, j])
        wait_here(s_in.at[way, h, j], s_recv.at[way, h, j])

    def pass_on(h, way):
        first, stop = (t + 1, team) if way == RIGHT else (0, t)
        is_source = t == 0 if way == RIGHT else t == last

        @pl.loop(first, stop)
        def _(j):
            @pl.when(is_source)
            def _():
                o_out[way, h, j] = part_o[h, j].astype(jnp.bfloat16)
                s_out[way, h, j] = part_s[h, j]

            @pl.when(jnp.logical_not(is_source))
            def _():
                await_partial(h, j, way)
                o, s = merge(
                    part_o[h, j], part_s[h, j],
                    o_in[way, h, j].astype(jnp.float32), s_in[way, h, j],
                )
                o_out[way, h, j] = o.astype(jnp.bfloat16)
                s_out[way, h, j] = s

            for copy in o_copy(h, j, way):
                copy.start()

    def finish(h):
        for way, present in ((RIGHT, t > 0), (LEFT, t < last)):
            @pl.when(present)
            def _():
                await_partial(h, t, way)
                o, s = merge(
                    part_o[h, t], part_s[h, t],
                    o_in[way, h, t].astype(jnp.float32), s_in[way, h, t],
                )
                part_o[h, t] = o
                part_s[h, t] = s

        out_ref[:, columns(h)] = part_o[h, t].T.astype(out_ref.dtype)

    def guarded(h, action):
        @pl.when(jnp.logical_and(h >= 0, h < heads))
        def _():
            action(h)

    @pl.loop(0, heads + 2 * last)
    def _(step):
        @pl.when(step < heads)
        def _():
            send_own_q(step)
            send_kv(step)

        for distance in range(1, team):
            guarded(step - distance, functools.partial(relay_q, distance=distance))
        now = step - last
        guarded(now, attend)
        guarded(now - t, functools.partial(pass_on, way=RIGHT))
        guarded(now - (last - t), functools.partial(pass_on, way=LEFT))
        guarded(now - last, finish)

    @pl.loop(0, heads)
    def _(h):
        if blk > 1:
            for which in range(2):
                wait_here(kvbuf.at[h, which, pl.ds(1, blk - 1)], kv_send.at[which, h])

        @pl.when(t > 0)
        def _():
            @pl.loop(t, team)
            def _(j):
                wait_here(qbuf.at[h, j], q_send.at[LEFT, h, j])

            @pl.loop(0, t)
            def _(j):
                wait_here(o_out.at[LEFT, h, j], o_send.at[LEFT, h, j])
                wait_here(s_out.at[LEFT, h, j], s_send.at[LEFT, h, j])

        @pl.when(t < last)
        def _():
            @pl.loop(0, t + 1)
            def _(j):
                wait_here(qbuf.at[h, j], q_send.at[RIGHT, h, j])

            @pl.loop(t + 1, team)
            def _(j):
                wait_here(o_out.at[RIGHT, h, j], o_send.at[RIGHT, h, j])
                wait_here(s_out.at[RIGHT, h, j], s_send.at[RIGHT, h, j])


def on_device(team, blk, query, keys, values):
    rows, width = query.shape
    heads = width // HEAD_DIM
    dma = pltpu.SemaphoreType.DMA
    bf16, f32 = jnp.bfloat16, jnp.float32
    return pl.pallas_call(
        functools.partial(kernel, team, blk),
        out_shape=jax.ShapeDtypeStruct((rows, width), query.dtype),
        in_specs=[pl.BlockSpec(memory_space=pltpu.VMEM)] * 3,
        out_specs=pl.BlockSpec(memory_space=pltpu.VMEM),
        scratch_shapes=[
            pltpu.VMEM((heads, team, rows, HEAD_DIM), bf16),
            pltpu.VMEM((heads, 2, blk, rows, HEAD_DIM), bf16),
            pltpu.VMEM((heads, team, HEAD_DIM, rows), f32),
            pltpu.VMEM((heads, team, 1, rows), f32),
            pltpu.VMEM((2, heads, team, HEAD_DIM, rows), bf16),
            pltpu.VMEM((2, heads, team, 1, rows), f32),
            pltpu.VMEM((2, heads, team, HEAD_DIM, rows), bf16),
            pltpu.VMEM((2, heads, team, 1, rows), f32),
            dma((heads, team)),
            dma((2, heads, team)),
            dma((2, heads)),
            dma((2, heads)),
            dma((2, heads, team)),
            dma((2, heads, team)),
            dma((2, heads, team)),
            dma((2, heads, team)),
        ],
        compiler_params=pltpu.CompilerParams(
            collective_id=0, has_side_effects=True, vmem_limit_bytes=60 * 1024 * 1024
        ),
    )(query, keys, values)


def solution(mesh):
    placed = P(("team", "blk"), "head")
    return jax.shard_map(
        functools.partial(on_device, mesh.shape["team"], mesh.shape["blk"]),
        mesh=mesh, in_specs=(placed,) * 3, out_specs=placed, check_vma=False,
    )
```

time: 163 us -> 62.9 us (0.39)
  waiting for transfers between devices: 81.8 us -> 0 us
  Pallas kernels: 0 us -> 61 us
  starting transfers between devices: 23.8 us -> 0 us
  matrix products: 19.9 us -> 0 us
  between operations: 13.7 us -> 0.01 us
  local copies, waits for them, and re-layouts: 14 us -> 1.72 us
  other arithmetic: 9.52 us -> 0 us
    pallas_call x0 -> x1, Pallas kernels: none -> 61 us  [on_device(): pl.pallas_call(functools.partial(kernel, team, blk), out_shape=jax.ShapeD...]
    all_to_all x3 -> x0, waiting for transfers between devices: 53.8 us -> none  [the longest x1 53.8 us: on_device(): lax.all_to_all(accumulated[None], 'team', split_axis=1, concat_axis=0, ti...]
    dot_general x8 -> x0, matrix products: 19.9 us -> none  [the longest x4 15.2 us: weighted(): jnp.einsum('qhk,khd->qhd', weights.astype(jnp.bfloat16), value_heads, pre...]
    all_to_all x3 -> x0, starting transfers between devices: 15.5 us -> none  [the longest x1 5.34 us: on_device(): lax.all_to_all(row_peak[None], 'team', split_axis=1, concat_axis=0, tiled...]
    all_gather x1 -> x0, waiting for transfers between devices: 14.8 us -> none  [on_device(): team_query = lax.all_gather(query, 'team', axis=0, tiled=True)]
    ppermute x6 -> x0, waiting for transfers between devices: 13.2 us -> none  [shifted(): lax.ppermute(value, axis, [(i, (i + by) % count) for i in range(count)])]
    ppermute x6 -> x0, starting transfers between devices: 8.25 us -> none  [shifted(): lax.ppermute(value, axis, [(i, (i + by) % count) for i in range(count)])]
    unnamed x37 -> x1, local copies, waits for them, and re-layouts: 8.02 us -> 1.72 us
  transfers between devices with their start and end apart: 10 -> 0, of which waited for: 5 -> 0; matrix products, arithmetic and copies ran while one was open for 24% -> 0% of each run, Pallas kernels for 0% -> 0%
where the time goes in v1:
time: 62.9 us; the launch traced here: 62.8 us
  Pallas kernels  61 us (97%)
  local copies, waits for them, and re-layouts  1.72 us (3%)
    pallas_call x1, Pallas kernels, on_device(): pl.pallas_call(functools.partial(kernel, team, blk), out_shape=jax.ShapeD...  61 us
    unnamed x1, local copies, waits for them, and re-layouts  1.72 us

profile of v1, /device:TPU:0, one launch (start us, length us, event | category | flops | bytes accessed | tf_op | source)
XLA Modules:
  0.0 62.8 jit_solution(11739706573693151048)
XLA Ops:
  0.0 61.0 %shard_map.37 = bf16[128,1280]{1,0:T(8,128)(2,1)} custom-call(bf16[128,1280]{1,0:T(8,128)(2,1)} %q_ref.1, bf16[128,1280]{1,0:T(8,128)(2,1)} %k_ref.1, bf16[128,1280]{1,0:T(8,128)(2,1)} %v_ref.1), custom_call_target="tpu_custom_call" | custom-call | tf_op jit(solution)/shard_map/pallas_call | solution.py:284
  61.1 1.7 %copy.5 = bf16[128,1280]{1,0:T(8,128)(2,1)} copy(bf16[128,1280]{1,0:T(8,128)(2,1)} %shard_map.37) | data formatting | bytes 655360

commit v2 on v1

--- a/solution.py
+++ b/solution.py
@@ -11,6 +11,8 @@
 HEAD_DIM = 128
 MESH = pl.DeviceIdType.MESH
 RIGHT, LEFT = 0, 1
+QUERY_LAG = 2
+PARTIAL_LAG = 2
 
 
 def merge(o1, s1, o2, s2):
@@ -24,8 +26,8 @@
 
 def kernel(
     team, blk, q_ref, k_ref, v_ref, out_ref,
-    qbuf, kvbuf, part_o, part_s, o_in, s_in, o_out, s_out,
-    q_recv, q_send, kv_recv, kv_send, o_recv, o_send, s_recv, s_send,
+    qbuf, kvbuf, part_o, part_s, o_in, s_in, o_out, s_out, pair_size,
+    local, q_recv, q_send, kv_recv, kv_send, o_recv, o_send, s_send,
 ):
     rows = q_ref.shape[0]
     heads = q_ref.shape[1] // HEAD_DIM
@@ -37,6 +39,21 @@
     def columns(h):
         return pl.ds(pl.multiple_of(h * HEAD_DIM, HEAD_DIM), HEAD_DIM)
 
+    def wait_here(ref, semaphore):
+        pltpu.make_async_copy(ref, ref, semaphore).wait()
+
+    def load(h):
+        return (
+            pltpu.make_async_copy(q_ref.at[:, columns(h)], qbuf.at[h, t], local.at[0]),
+            pltpu.make_async_copy(k_ref.at[:, columns(h)], kvbuf.at[h, 0, 0], local.at[1]),
+            pltpu.make_async_copy(v_ref.at[:, columns(h)], kvbuf.at[h, 1, 0], local.at[2]),
+        )
+
+    @pl.loop(0, heads)
+    def _(h):
+        for copy in load(h):
+            copy.start()
+
     barrier = pltpu.get_barrier_semaphore()
 
     @pl.loop(1, blk)
@@ -55,14 +72,16 @@
 
     ends = jnp.where(t > 0, 1, 0) + jnp.where(t < last, 1, 0)
     pl.semaphore_wait(barrier, blk - 1 + ends)
+    wait_here(qbuf.at[:, t], local.at[0])
+    wait_here(kvbuf.at[:, 0, 0], local.at[1])
+    wait_here(kvbuf.at[:, 1, 0], local.at[2])
 
     def kv_copy(h, which, r):
-        source = (k_ref, v_ref)[which]
         return pltpu.make_async_remote_copy(
-            src_ref=source.at[:, columns(h)],
+            src_ref=kvbuf.at[h, which, 0],
             dst_ref=kvbuf.at[h, which, r],
-            send_sem=kv_send.at[which, h],
-            recv_sem=kv_recv.at[which, h],
+            send_sem=kv_send.at[0],
+            recv_sem=kv_recv.at[h],
             device_id={"blk": lax.rem(b + r, blk)},
             device_id_type=MESH,
         )
@@ -72,7 +91,7 @@
         return pltpu.make_async_remote_copy(
             src_ref=source,
             dst_ref=qbuf.at[h, j],
-            send_sem=q_send.at[way, h, j],
+            send_sem=q_send.at[way, j],
             recv_sem=q_recv.at[h, j],
             device_id={"team": target},
             device_id_type=MESH,
@@ -83,17 +102,17 @@
         return (
             pltpu.make_async_remote_copy(
                 src_ref=o_out.at[way, h, j],
-                dst_ref=o_in.at[way, h, j],
-                send_sem=o_send.at[way, h, j],
-                recv_sem=o_recv.at[way, h, j],
+                dst_ref=o_in.at[h, j + 1 - way],
+                send_sem=o_send.at[way, j],
+                recv_sem=o_recv.at[h, j + 1 - way],
                 device_id={"team": target},
                 device_id_type=MESH,
             ),
             pltpu.make_async_remote_copy(
                 src_ref=s_out.at[way, h, j],
-                dst_ref=s_in.at[way, h, j],
-                send_sem=s_send.at[way, h, j],
-                recv_sem=s_recv.at[way, h, j],
+                dst_ref=s_in.at[h, j + 1 - way],
+                send_sem=s_send.at[way, j],
+                recv_sem=o_recv.at[h, j + 1 - way],
                 device_id={"team": target},
                 device_id_type=MESH,
             ),
@@ -108,14 +127,11 @@
     def send_own_q(h):
         @pl.when(t > 0)
         def _():
-            q_copy(q_ref.at[:, columns(h)], h, t, LEFT).start()
+            q_copy(qbuf.at[h, t], h, t, LEFT).start()
 
         @pl.when(t < last)
         def _():
-            q_copy(q_ref.at[:, columns(h)], h, t, RIGHT).start()
-
-    def wait_here(ref, semaphore):
-        pltpu.make_async_copy(ref, ref, semaphore).wait()
+            q_copy(qbuf.at[h, t], h, t, RIGHT).start()
 
     def relay_q(h, distance):
         @pl.when(t + distance <= last)
@@ -140,13 +156,9 @@
     groups = blk // group
 
     def attend(h):
-        qbuf[h, t] = q_ref[:, columns(h)]
-        kvbuf[h, 0, 0] = k_ref[:, columns(h)]
-        kvbuf[h, 1, 0] = v_ref[:, columns(h)]
         queries = qbuf[h].reshape(team * rows, HEAD_DIM)
-        for which in range(2):
-            if blk > 1:
-                wait_here(kvbuf.at[h, which, pl.ds(1, blk - 1)], kv_recv.at[which, h])
+        if blk > 1:
+            wait_here(kvbuf.at[h, :, pl.ds(1, blk - 1)], kv_recv.at[h])
 
         def scores_of(c):
             keys = kvbuf[h, 0, pl.ds(c * group, group)].reshape(group * rows, HEAD_DIM)
@@ -186,15 +198,16 @@
             part_s[h, j] = level[:, j * rows : (j + 1) * rows]
 
     def await_partial(h, j, way):
-        wait_here(o_in.at[way, h, j], o_recv.at[way, h, j])
-        wait_here(s_in.at[way, h, j], s_recv.at[way, h, j])
+        wait_here(pair_size, o_recv.at[h, j + 1 - way])
 
     def pass_on(h, way):
         first, stop = (t + 1, team) if way == RIGHT else (0, t)
         is_source = t == 0 if way == RIGHT else t == last
 
         @pl.loop(first, stop)
-        def _(j):
+        def _(index):
+            j = stop - 1 - (index - first) if way == RIGHT else index
+
             @pl.when(is_source)
             def _():
                 o_out[way, h, j] = part_o[h, j].astype(jnp.bfloat16)
@@ -205,7 +218,7 @@
                 await_partial(h, j, way)
                 o, s = merge(
                     part_o[h, j], part_s[h, j],
-                    o_in[way, h, j].astype(jnp.float32), s_in[way, h, j],
+                    o_in[h, j + 1 - way].astype(jnp.float32), s_in[h, j + 1 - way],
                 )
                 o_out[way, h, j] = o.astype(jnp.bfloat16)
                 s_out[way, h, j] = s
@@ -220,7 +233,7 @@
                 await_partial(h, t, way)
                 o, s = merge(
                     part_o[h, t], part_s[h, t],
-                    o_in[way, h, t].astype(jnp.float32), s_in[way, h, t],
+                    o_in[h, t + 1 - way].astype(jnp.float32), s_in[h, t + 1 - way],
                 )
                 part_o[h, t] = o
                 part_s[h, t] = s
@@ -232,7 +245,7 @@
         def _():
             action(h)
 
-    @pl.loop(0, heads + 2 * last)
+    @pl.loop(0, heads + (QUERY_LAG + PARTIAL_LAG) * last)
     def _(step):
         @pl.when(step < heads)
         def _():
@@ -240,40 +253,35 @@
             send_kv(step)
 
         for distance in range(1, team):
-            guarded(step - distance, functools.partial(relay_q, distance=distance))
-        now = step - last
+            guarded(
+                step - QUERY_LAG * distance, functools.partial(relay_q, distance=distance)
+            )
+        now = step - QUERY_LAG * last
         guarded(now, attend)
-        guarded(now - t, functools.partial(pass_on, way=RIGHT))
-        guarded(now - (last - t), functools.partial(pass_on, way=LEFT))
-        guarded(now - last, finish)
-
-    @pl.loop(0, heads)
-    def _(h):
-        if blk > 1:
-            for which in range(2):
-                wait_here(kvbuf.at[h, which, pl.ds(1, blk - 1)], kv_send.at[which, h])
-
-        @pl.when(t > 0)
-        def _():
-            @pl.loop(t, team)
-            def _(j):
-                wait_here(qbuf.at[h, j], q_send.at[LEFT, h, j])
-
-            @pl.loop(0, t)
-            def _(j):
-                wait_here(o_out.at[LEFT, h, j], o_send.at[LEFT, h, j])
-                wait_here(s_out.at[LEFT, h, j], s_send.at[LEFT, h, j])
-
-        @pl.when(t < last)
-        def _():
-            @pl.loop(0, t + 1)
-            def _(j):
-                wait_here(qbuf.at[h, j], q_send.at[RIGHT, h, j])
-
-            @pl.loop(t + 1, team)
-            def _(j):
-                wait_here(o_out.at[RIGHT, h, j], o_send.at[RIGHT, h, j])
-                wait_here(s_out.at[RIGHT, h, j], s_send.at[RIGHT, h, j])
+        guarded(now - PARTIAL_LAG * t, functools.partial(pass_on, way=RIGHT))
+        guarded(now - PARTIAL_LAG * (last - t), functools.partial(pass_on, way=LEFT))
+        guarded(now - PARTIAL_LAG * last, finish)
+
+    if blk > 1:
+        wait_here(kvbuf.at[:, :, pl.ds(1, blk - 1)], kv_send.at[0])
+
+    def drain(way, first_q, stop_q, first_o, stop_o):
+        @pl.loop(first_q, stop_q)
+        def _(j):
+            wait_here(qbuf.at[:, j], q_send.at[way, j])
+
+        @pl.loop(first_o, stop_o)
+        def _(j):
+            wait_here(o_out.at[way, :, j], o_send.at[way, j])
+            wait_here(s_out.at[way, :, j], s_send.at[way, j])
+
+    @pl.when(t > 0)
+    def _():
+        drain(LEFT, t, team, 0, t)
+
+    @pl.when(t < last)
+    def _():
+        drain(RIGHT, 0, t + 1, t + 1, team)
 
 
 def on_device(team, blk, query, keys, values):
@@ -284,25 +292,26 @@
     return pl.pallas_call(
         functools.partial(kernel, team, blk),
         out_shape=jax.ShapeDtypeStruct((rows, width), query.dtype),
-        in_specs=[pl.BlockSpec(memory_space=pltpu.VMEM)] * 3,
+        in_specs=[pl.BlockSpec(memory_space=pl.ANY)] * 3,
         out_specs=pl.BlockSpec(memory_space=pltpu.VMEM),
         scratch_shapes=[
             pltpu.VMEM((heads, team, rows, HEAD_DIM), bf16),
             pltpu.VMEM((heads, 2, blk, rows, HEAD_DIM), bf16),
             pltpu.VMEM((heads, team, HEAD_DIM, rows), f32),
             pltpu.VMEM((heads, team, 1, rows), f32),
+            pltpu.VMEM((heads, team + 1, HEAD_DIM, rows), bf16),
+            pltpu.VMEM((heads, team + 1, 1, rows), f32),
             pltpu.VMEM((2, heads, team, HEAD_DIM, rows), bf16),
             pltpu.VMEM((2, heads, team, 1, rows), f32),
-            pltpu.VMEM((2, heads, team, HEAD_DIM, rows), bf16),
-            pltpu.VMEM((2, heads, team, 1, rows), f32),
+            pltpu.VMEM((HEAD_DIM // 2 + 1, 1, rows), f32),
+            dma((3,)),
             dma((heads, team)),
-            dma((2, heads, team)),
-            dma((2, heads)),
-            dma((2, heads)),
-            dma((2, heads, team)),
-            dma((2, heads, team)),
-            dma((2, heads, team)),
-            dma((2, heads, team)),
+            dma((2, team)),
+            dma((heads,)),
+            dma((1,)),
+            dma((heads, team + 1)),
+            dma((2, team)),
+            dma((2, team)),
         ],
         compiler_params=pltpu.CompilerParams(
             collective_id=0, has_side_effects=True, vmem_limit_bytes=60 * 1024 * 1024

time: 62.9 us -> 48.9 us (0.78)
  Pallas kernels: 61 us -> 47 us
    pallas_call x1, Pallas kernels: 61 us -> 47 us  [on_device(): pl.pallas_call(functools.partial(kernel, team, blk), out_shape=jax.ShapeD...]
where the time goes in v2:
time: 48.9 us; the launch traced here: 48.7 us
  Pallas kernels  47 us (96%)
  local copies, waits for them, and re-layouts  1.72 us (4%)
    pallas_call x1, Pallas kernels, on_device(): pl.pallas_call(functools.partial(kernel, team, blk), out_shape=jax.ShapeD...  47 us
    unnamed x1, local copies, waits for them, and re-layouts  1.72 us

profile of v2, /device:TPU:0, one launch (start us, length us, event | category | flops | bytes accessed | tf_op | source)
XLA Modules:
  0.0 48.7 jit_solution(4738321671955636943)
XLA Ops:
  0.0 47.0 %shard_map.37 = bf16[128,1280]{1,0:T(8,128)(2,1)} custom-call(bf16[128,1280]{1,0:T(8,128)(2,1)} %q_ref.1, bf16[128,1280]{1,0:T(8,128)(2,1)} %k_ref.1, bf16[128,1280]{1,0:T(8,128)(2,1)} %v_ref.1), custom_call_target="tpu_custom_call" | custom-call | tf_op jit(solution)/shard_map/pallas_call | solution.py:292
  47.0 1.7 %copy.5 = bf16[128,1280]{1,0:T(8,128)(2,1)} copy(bf16[128,1280]{1,0:T(8,128)(2,1)} %shard_map.37) | data formatting | bytes 655360

commit v3 on v2

--- a/solution.py
+++ b/solution.py
@@ -76,10 +76,10 @@
     wait_here(kvbuf.at[:, 0, 0], local.at[1])
     wait_here(kvbuf.at[:, 1, 0], local.at[2])
 
-    def kv_copy(h, which, r):
+    def kv_copy(h, r):
         return pltpu.make_async_remote_copy(
-            src_ref=kvbuf.at[h, which, 0],
-            dst_ref=kvbuf.at[h, which, r],
+            src_ref=kvbuf.at[h, :, 0],
+            dst_ref=kvbuf.at[h, :, r],
             send_sem=kv_send.at[0],
             recv_sem=kv_recv.at[h],
             device_id={"blk": lax.rem(b + r, blk)},
@@ -119,10 +119,9 @@
         )
 
     def send_kv(h):
-        for which in range(2):
-            @pl.loop(1, blk)
-            def _(r):
-                kv_copy(h, which, r).start()
+        @pl.loop(1, blk)
+        def _(r):
+            kv_copy(h, r).start()
 
     def send_own_q(h):
         @pl.when(t > 0)

time: 48.9 us -> 48.9 us (level)
  no operation moved by 1% of the time
where the time goes in v3:
time: 48.9 us; the launch traced here: 48.7 us
  Pallas kernels  47 us (96%)
  local copies, waits for them, and re-layouts  1.72 us (4%)
    pallas_call x1, Pallas kernels, on_device(): pl.pallas_call(functools.partial(kernel, team, blk), out_shape=jax.ShapeD...  47 us
    unnamed x1, local copies, waits for them, and re-layouts  1.72 us

profile of v3, /device:TPU:0, one launch (start us, length us, event | category | flops | bytes accessed | tf_op | source)
XLA Modules:
  0.0 48.7 jit_solution(7557904106889153928)
XLA Ops:
  0.0 47.0 %shard_map.37 = bf16[128,1280]{1,0:T(8,128)(2,1)} custom-call(bf16[128,1280]{1,0:T(8,128)(2,1)} %q_ref.1, bf16[128,1280]{1,0:T(8,128)(2,1)} %k_ref.1, bf16[128,1280]{1,0:T(8,128)(2,1)} %v_ref.1), custom_call_target="tpu_custom_call" | custom-call | tf_op jit(solution)/shard_map/pallas_call | solution.py:291
  47.0 1.7 %copy.5 = bf16[128,1280]{1,0:T(8,128)(2,1)} copy(bf16[128,1280]{1,0:T(8,128)(2,1)} %shard_map.37) | data formatting | bytes 655360
